TPU v7x, 256 devices: a whole 4x4x8 slice. The times are simulated.
256 devices in a mesh: gx: 16 (over z_hi, y, core), gy: 16 (over x, z_lo).
Axes of the slice: x: 4, y: 4, z: 8 (z_hi: 2, z_lo: 4; z = z_hi * 4 + z_lo), core: 2. Of those that a mesh axis runs over, the one named last changes fastest.
Arguments:
- adjoint_rhs: float32 [32, 16, 768, 128], P('gx', 'gy'), may hold values from -6 to 6
- local_inverse: bfloat16 [32, 16, 1024, 768], P('gx', 'gy')
- local_operator: bfloat16 [32, 16, 1024, 768], P('gx', 'gy')
- spill_rows: int32 [32, 16, 4, 64], P('gx', 'gy'), may hold values from 0 to 767, as said below
- coarse_basis: bfloat16 [32, 16, 64, 768], P('gx', 'gy'), may hold values from -3 to 3
- coarse_ids: int32 [32, 16, 64], P('gx', 'gy'), may hold values from 0 to 1023
- coarse_inverse: bfloat16 [1024, 1024], P(('gx', 'gy')), may hold values from -0.00030517578 to 0.00030517578
Outputs:
- adjoint_solution: float32 [32, 16, 768, 128], P('gx', 'gy')
- residual: float32 [32, 16, 768, 128], P('gx', 'gy')
Inputs may be any that keep to these rules, and one draw needn't show every extreme that they name: Each list of spill_rows holds 64 distinct rows. `coarse_ids`: A coarse function may be listed more than once for a subdomain.
All inputs are finite; a program needn't handle non-finite values.
Results may differ from a plain program's by a relative error of at most 0.0041.
Values may be sent and summed in bfloat16 or wider, within the bound.
A program may use at most 64 MiB of HBM per device.

v0:
```python
import jax
import jax.numpy as jnp
from jax import lax
from jax.sharding import PartitionSpec as P


def with_halo(block, sides, width):
    for axis, dim in sides:
        count = lax.axis_size(axis)
        forward = [(i, i + 1) for i in range(count - 1)]
        backward = [(target, source) for source, target in forward]
        low = lax.ppermute(
            lax.slice_in_dim(block, block.shape[dim] - width, None, axis=dim), axis, forward
        )
        high = lax.ppermute(lax.slice_in_dim(block, 0, width, axis=dim), axis, backward)
        block = jnp.concatenate([low, block, high], axis=dim)
    return block


def add_rows(owned_rows, indices, values):
    return owned_rows.at[indices].add(values)


def spread(extended, indices):
    sub_count = extended.shape[0]
    group_rows = indices.shape[1] // 4
    owned_count = extended.shape[1] - 4 * group_rows
    owned_rows = extended[:, :owned_count]
    groups = extended[:, owned_count:].reshape(sub_count, 4, group_rows, extended.shape[2])
    outward = jnp.stack([groups[0, 0], groups[sub_count - 1, 1]])
    across = with_halo(outward, (("gx", 0),), 1)
    from_west = jnp.concatenate([across[0][None], groups[:-1, 1]], 0)
    from_east = jnp.concatenate([groups[1:, 0], across[3][None]], 0)
    vertical = jnp.stack([groups[:, 2], groups[:, 3]])
    beside = with_halo(vertical, (("gy", 0),), 1)
    received = jnp.stack([from_west, from_east, beside[0], beside[3]], 1).reshape(
        sub_count, 4 * group_rows, extended.shape[2]
    )
    return jax.vmap(add_rows)(owned_rows, indices, received)


def body(
    adjoint_rhs, local_inverse, local_operator, spill_rows, coarse_basis, coarse_ids, coarse_inverse
):
    highest = lax.Precision.HIGHEST
    contract_first = (((0,), (0,)), ((), ()))
    residual = adjoint_rhs[:, 0]
    inverses = local_inverse[:, 0]
    operators = local_operator[:, 0]
    indices = spill_rows[:, 0].reshape(spill_rows.shape[0], -1)
    basis_rows = coarse_basis[:, 0].astype(jnp.float32)
    sub_count = coarse_ids.shape[0]
    functions = coarse_ids.shape[2]
    coarse_order = coarse_inverse.shape[1]
    flat_ids = coarse_ids[:, 0].reshape(-1)
    one_hot = (flat_ids[None, :] == jnp.arange(coarse_order, dtype=jnp.int32)[:, None]).astype(
        jnp.float32
    )
    terms = jnp.einsum("skn,snr->skr", basis_rows, residual, precision=highest)
    local_sums = jnp.dot(
        one_hot, terms.reshape(sub_count * functions, terms.shape[2]), precision=highest
    )
    shares = lax.psum_scatter(local_sums, ("gx", "gy"), scatter_dimension=0, tiled=True)
    partial_sol = lax.dot_general(
        coarse_inverse,
        shares.astype(jnp.bfloat16),
        contract_first,
        preferred_element_type=jnp.float32,
    )
    coarse_sol = lax.psum(partial_sol, ("gx", "gy"))
    local_sol = jnp.einsum(
        "sln,snr->slr", inverses, residual.astype(jnp.bfloat16), preferred_element_type=jnp.float32
    )
    picked = jnp.dot(one_hot.T, coarse_sol, precision=highest).reshape(
        sub_count, functions, coarse_sol.shape[1]
    )
    coarse_part = jnp.einsum("skn,skr->snr", basis_rows, picked, precision=highest)
    correction = spread(local_sol, indices) + coarse_part
    image = jnp.einsum(
        "sln,snr->slr",
        operators,
        correction.astype(jnp.bfloat16),
        preferred_element_type=jnp.float32,
    )
    residual = residual - spread(image, indices)
    return (correction[:, None], residual[:, None])


def solution(mesh):
    in_specs = (
        P("gx", "gy", None, None),
        P("gx", "gy", None, None),
        P("gx", "gy", None, None),
        P("gx", "gy", None, None),
        P("gx", "gy", None, None),
        P("gx", "gy", None),
        P(("gx", "gy"), None),
    )
    out_specs = (P("gx", "gy", None, None), P("gx", "gy", None, None))
    return jax.shard_map(body, mesh=mesh, in_specs=in_specs, out_specs=out_specs, check_vma=False)
```

profile of v0, /device:TPU:1, one launch (start us, length us, event | category | flops | bytes accessed | tf_op | source)
XLA Modules:
  0.0 494.6 jit_solution(17594343954247628550)
XLA Ops:
  7.2 0.0 copy-start
  7.2 0.0 all-reduce.4.cloned.1.call-start
  7.2 0.5 broadcast.62
  7.7 1.6 reduce.3
  9.4 0.1 eq.15
  9.5 1.6 fusion.8
  11.1 1.2 fusion.12
  12.3 82.9 %all-reduce.5 = bf16[1024,128]{1,0:T(8,128)(2,1)S(1)} all-reduce(f32[1024,128]{1,0:T(8,128)} %fusion.12), channel_id=2, replica_groups=mesh['gx'=16,'gy'=16] {'gx','gy'}, use_global_device_ids=true, to_apply=%region_0.0.clone | all-reduce | flops 131072 | bytes 786432
  95.2 1.8 convolution_bitcast_fusion.1
  97.0 0.0 all-reduce.4.cloned.1.call-update
  97.0 0.0 copy-done
  97.0 0.0 copy-start.5
  97.0 2.1 fusion.2
  99.2 0.0 copy-start.1
  99.2 1.0 copy-done.1
  100.2 0.6 slice_bitcast_fusion.11
  100.8 1.9 collective-permute-start
  102.7 2.4 collective-permute-start.1
  105.1 2.7 collective-permute-start.2
  107.8 1.3 collective-permute-start.3
  109.1 0.0 copy-done.5
  109.1 0.1 reshape_squeeze.3
  109.2 0.0 collective-permute-done
  109.2 0.0 collective-permute-done.1
  109.3 0.4 collective-permute-done.2
  109.7 5.6 %collective-permute-done.3 = f32[1,2,64,128]{3,2,1,0:T(8,128)S(1)} collective-permute-done((f32[1,2,64,128]{3,2,1,0:T(8,128)S(1)}, f32[1,2,64,128]{3,2,1,0:T(8,128)S(1)}, u32[]{:S(2)}, u32[]{:S(2)}) %collective-permute-start.3) | collective-permute-done | bytes 65568 | tf_op jit(solution)/shard_map/ppermute | solution.py:15
  115.4 232.7 %all-reduce.4.cloned.1.call-done = f32[1024,128]{0,1:T(8,128)} async-done(((f32[1024,128]{0,1:T(8,128)}), f32[1024,128]{0,1:T(8,128)}) %all-reduce.4.cloned.1.call-update) | async-done | bytes 524304 | tf_op jit(solution)/shard_map/psum | solution.py:70
  348.1 1.5 fusion.14
  349.6 2.7 fusion.7
  352.3 54.2 %scatter_fusion = f32[2,768,128]{2,1,0:T(8,128)} fusion(f32[2,768,128]{2,1,0:T(8,128)} %fusion.7, s32[512]{0:T(512)S(1)} %bitcast.99, f32[512,128]{1,0:T(8,128)S(1)} %bitcast.102), kind=kCustom, calls=%fused_computation | custom fusion | flops 65536 | bytes 790528 | tf_op jit(solution)/shard_map/vmap()/scatter-add | solution.py:21
  406.5 3.3 fusion.4
  409.8 0.0 copy-start.2
  409.8 1.0 copy-done.2
  410.8 0.7 slice.77
  411.5 1.1 copy.38
  412.6 0.6 slice_bitcast_fusion.7
  413.2 5.1 %collective-permute-start.4 = (f32[1,64,128]{2,1,0:T(8,128)}, f32[1,64,128]{2,1,0:T(8,128)}, u32[]{:S(2)}, u32[]{:S(2)}) collective-permute-start(f32[1,64,128]{2,1,0:T(8,128)} %get-tuple-element.8), channel_id=1, source_target_pairs={{0,16},{16,32},{32,48},{48,64},{64,80},{80,96},{96,112},{112,128},... | collective-permute-start | bytes 98312 | tf_op jit(solution)/shard_map/ppermute | solution.py:12
  418.3 0.6 slice_bitcast_fusion.1
  418.9 0.0 copy-start.4
  418.9 0.0 copy-start.3
  418.9 2.1 slice.76
  421.0 2.3 copy.41
  423.3 0.0 copy-done.4
  423.3 1.9 collective-permute-start.5
  425.3 0.0 copy-done.3
  425.3 1.3 collective-permute-start.6
  426.6 1.3 collective-permute-start.7
  427.9 0.0 collective-permute-done.4
  427.9 0.8 maximum_bitcast_fusion.2
  428.6 0.0 collective-permute-done.5
  428.7 0.0 collective-permute-done.6
  428.7 5.6 %collective-permute-done.7 = f32[1,2,64,128]{3,2,1,0:T(8,128)S(1)} collective-permute-done((f32[1,2,64,128]{3,2,1,0:T(8,128)S(1)}, f32[1,2,64,128]{3,2,1,0:T(8,128)S(1)}, u32[]{:S(2)}, u32[]{:S(2)}) %collective-permute-start.7) | collective-permute-done | bytes 65568 | tf_op jit(solution)/shard_map/ppermute | solution.py:15
  434.3 51.2 %scatter_fusion.1 = f32[2,768,128]{2,1,0:T(8,128)} fusion(f32[2,768,128]{2,1,0:T(8,128)} %copy.41, s32[512]{0:T(512)S(1)} %bitcast.100, f32[512,128]{1,0:T(8,128)S(1)} %bitcast.103), kind=kCustom, calls=%fused_computation.1 | custom fusion | flops 65536 | bytes 790528 | tf_op jit(solution)/shard_map/vmap()/scatter-add | solution.py:21
  485.5 2.3 fusion.10
  (11 shorter events, 0.1 us)
Async XLA Ops:
  7.2 89.9 %copy-start = (bf16[2,1,1024,768]{3,2,1,0:T(8,128)(2,1)S(1)}, bf16[2,1,1024,768]{3,2,1,0:T(8,128)(2,1)}, u32[]{:S(2)}) copy-start(bf16[2,1,1024,768]{3,2,1,0:T(8,128)(2,1)} %param.8) | copy-start | bytes 9437188
  7.2 340.9 %all-reduce.4.cloned.1.call-start = ((), (), s32[]{:S(2)}) async-start(), calls=%async_computation | async-start | bytes 1048576 | tf_op jit(solution)/shard_map/psum | solution.py:70
  97.0 12.1 %copy-start.5 = (s32[2,1,4,64]{3,2,1,0:T(4,128)S(1)}, s32[2,1,4,64]{3,2,1,0:T(4,128)}, u32[]{:S(2)}) copy-start(s32[2,1,4,64]{3,2,1,0:T(4,128)} %param.10) | copy-start | bytes 6148
  99.2 1.0 copy-start.1
  100.8 8.4 %collective-permute-start = (f32[1,64,128]{2,1,0:T(8,128)}, f32[1,64,128]{2,1,0:T(8,128)S(1)}, u32[]{:S(2)}, u32[]{:S(2)}) collective-permute-start(f32[1,64,128]{2,1,0:T(8,128)} %get-tuple-element.14), channel_id=1, source_target_pairs={{0,16},{16,32},{32,48},{48,64},{64,80},{80,96},{96,112},{112,128},... | collective-permute-start | bytes 98312 | tf_op jit(solution)/shard_map/ppermute | solution.py:12
  102.7 6.5 %collective-permute-start.1 = (f32[1,64,128]{2,1,0:T(8,128)}, f32[1,64,128]{2,1,0:T(8,128)S(1)}, u32[]{:S(2)}, u32[]{:S(2)}) collective-permute-start(f32[1,64,128]{2,1,0:T(8,128)} %get-tuple-element.15), channel_id=1, source_target_pairs={{16,0},{32,16},{48,32},{64,48},{80,64},{96,80},{112,96},{128,112},... | collective-permute-start | bytes 98312 | tf_op jit(solution)/shard_map/ppermute | solution.py:15
  105.1 4.5 collective-permute-start.2
  107.8 7.5 %collective-permute-start.3 = (f32[1,2,64,128]{3,2,1,0:T(8,128)S(1)}, f32[1,2,64,128]{3,2,1,0:T(8,128)S(1)}, u32[]{:S(2)}, u32[]{:S(2)}) collective-permute-start(f32[1,2,64,128]{3,2,1,0:T(8,128)S(1)} %get-tuple-element.19), channel_id=1, source_target_pairs={{1,0},{2,1},{3,2},{4,3},{5,4},{6,5},{7,6},{8,7},{9,8},{10,9},{11,1... | collective-permute-start | bytes 196616 | tf_op jit(solution)/shard_map/ppermute | solution.py:15
  409.8 1.0 copy-start.2
  413.2 14.7 %collective-permute-start.4 = (f32[1,64,128]{2,1,0:T(8,128)}, f32[1,64,128]{2,1,0:T(8,128)}, u32[]{:S(2)}, u32[]{:S(2)}) collective-permute-start(f32[1,64,128]{2,1,0:T(8,128)} %get-tuple-element.8), channel_id=1, source_target_pairs={{0,16},{16,32},{32,48},{48,64},{64,80},{80,96},{96,112},{112,128},... | collective-permute-start | bytes 98312 | tf_op jit(solution)/shard_map/ppermute | solution.py:12
  418.9 4.4 copy-start.4
  418.9 6.3 %copy-start.3 = (f32[1,2,64,128]{3,2,1,0:T(8,128)S(1)}, f32[1,2,64,128]{3,2,1,0:T(8,128)}, u32[]{:S(2)}) copy-start(f32[1,2,64,128]{3,2,1,0:T(8,128)} %get-tuple-element.12) | copy-start | bytes 196612
  423.3 5.3 %collective-permute-start.5 = (f32[1,64,128]{2,1,0:T(8,128)S(1)}, f32[1,64,128]{2,1,0:T(8,128)S(1)}, u32[]{:S(2)}, u32[]{:S(2)}) collective-permute-start(f32[1,64,128]{2,1,0:T(8,128)S(1)} %copy-done.4), channel_id=1, source_target_pairs={{16,0},{32,16},{48,32},{64,48},{80,64},{96,80},{112,96},{128,112},... | collective-permute-start | bytes 98312 | tf_op jit(solution)/shard_map/ppermute | solution.py:15
  425.3 3.4 collective-permute-start.6
  426.6 7.7 %collective-permute-start.7 = (f32[1,2,64,128]{3,2,1,0:T(8,128)S(1)}, f32[1,2,64,128]{3,2,1,0:T(8,128)S(1)}, u32[]{:S(2)}, u32[]{:S(2)}) collective-permute-start(f32[1,2,64,128]{3,2,1,0:T(8,128)S(1)} %get-tuple-element.13), channel_id=1, source_target_pairs={{1,0},{2,1},{3,2},{4,3},{5,4},{6,5},{7,6},{8,7},{9,8},{10,9},{11,1... | collective-permute-start | bytes 196616 | tf_op jit(solution)/shard_map/ppermute | solution.py:15
Sparse Core Ops, SparseCore 0:
  97.1 250.9 all-reduce.3
where the time goes:
time: 504 us; the launch traced here: 495 us
  waiting for transfers between devices  244 us (48%)
  other arithmetic  110 us (22%)
  blocking collectives  82.9 us (16%)
  starting transfers between devices  17.9 us (4%)
  between operations  14.3 us (3%)
  matrix products  14.2 us (3%)
  local copies, waits for them, and re-layouts  10.8 us (2%)
    psum x1, waiting for transfers between devices, body(): coarse_sol = lax.psum(partial_sol, ('gx', 'gy'))  233 us
    scatter-add x2, other arithmetic, add_rows(): return owned_rows.at[indices].add(values)  105 us
    unnamed x1, blocking collectives  82.9 us
    ppermute x4, waiting for transfers between devices, with_halo(): lax.ppermute(lax.slice_in_dim(block, 0, width, axis=dim), axis, backward)  11.2 us
    ppermute x4, starting transfers between devices, with_halo(): lax.ppermute(lax.slice_in_dim(block, block.shape[dim] - width, None, axis...  11 us
  transfers between devices with their start and end apart: 9, of which 4 were waited for; matrix products, arithmetic and copies ran while one was open for 2% of the time, Pallas kernels for 0%

commit v1 on v0

v1 whole, which is shorter than its diff:
```python
import functools

import jax
import jax.numpy as jnp
from jax import lax
from jax.experimental import pallas as pl
from jax.experimental.pallas import tpu as pltpu
from jax.sharding import PartitionSpec as P

F32 = jnp.float32
BF16 = jnp.bfloat16
MESH = pl.DeviceIdType.MESH
OWN = 768
H = 64
R = 128
KC = 64
NC = 1024
XS, YS, ZS = 4, 4, 8


def dot(a, b):
    return jnp.dot(a, b, preferred_element_type=F32)


def dot_first(a, b):
    return lax.dot_general(a, b, (((0,), (0,)), ((), ())), preferred_element_type=F32)


def split(value):
    high = value.astype(BF16)
    return high, (value - high.astype(F32)).astype(BF16)


def ring_distance(step, size):
    return min(step, size - step)


PLANE = sorted(
    [(dx, dy, dc) for dx in range(XS) for dy in range(YS) for dc in range(2) if (dx, dy, dc) != (0, 0, 0)],
    key=lambda o: -(ring_distance(o[0], XS) + ring_distance(o[1], YS)),
)
RING = sorted(range(1, ZS), key=lambda dz: -ring_distance(dz, ZS))


def kernel(
    rhs_hbm, inv_hbm, op_hbm, spill_hbm, basis_hbm, ids_hbm, cinv_hbm,
    sol_hbm, res_hbm,
    rhs, inv, op, spill, basis, ids, cz, cf,
    sbuf, rbuf, zs, zr, low,
    mbuf, marg, mbuf2, marg2, spread_mat, basis_t, wsel,
    corr, out_sol, out_res,
    load_sem, rs_send, rs_recv, z_send, z_recv, ag_send, ag_recv,
    cz_send, cz_recv, c2_send, c2_recv, c3_send, c3_recv, c4_send, c4_recv,
    m_send, m_recv, n_send, n_recv, store_sem,
):
    gx, gy = lax.axis_index("gx"), lax.axis_index("gy")
    core = lax.rem(gx, 2)
    y = lax.rem(lax.div(gx, 2), YS)
    x = lax.div(gy, 4)
    z = lax.div(gx, 8) * 4 + lax.rem(gy, 4)

    def device(xx, yy, zz, cc):
        return (lax.div(zz, 4) * 8 + yy * 2 + cc, xx * 4 + lax.rem(zz, 4))

    def plane_peer(offset):
        dx, dy, dc = offset
        xx, yy, cc = lax.rem(x + dx, XS), lax.rem(y + dy, YS), lax.rem(core + dc, 2)
        return (yy * 2 + cc) * 4 + xx, device(xx, yy, z, cc)

    def ring_peer(dz):
        return device(x, y, lax.rem(z + dz, ZS), core)

    def x_peer(dx):
        return device(lax.rem(x + dx, XS), y, z, core)

    def y_peer(dy):
        return device(x, lax.rem(y + dy, YS), z, core)

    partner = (gx + 1 - 2 * core, gy)
    east = (lax.rem(gx + 1, 16), gy)
    west = (lax.rem(gx + 15, 16), gy)
    north = (gx, lax.rem(gy + 1, 16))
    south = (gx, lax.rem(gy + 15, 16))
    mine = (y * 2 + core) * 4 + x

    def load(source, target, index):
        copy = pltpu.make_async_copy(source, target, load_sem.at[index])
        copy.start()
        return copy

    load_ids = load(ids_hbm, ids, 0)
    load_rhs = load(rhs_hbm, rhs, 1)
    load_basis = load(basis_hbm, basis, 2)
    load_cinv = load(cinv_hbm, cz.at[z], 3)
    load_inv = load(inv_hbm, inv, 4)
    load_spill = load(spill_hbm, spill, 5)
    load_op = load(op_hbm, op, 6)

    barrier = pltpu.get_barrier_semaphore()
    greeted = [plane_peer(o)[1] for o in PLANE] + [ring_peer(d) for d in RING] + [east, west, north, south]
    for peer in greeted:
        pl.semaphore_signal(barrier, inc=1, device_id=peer, device_id_type=MESH)

    def send(source, target, send_sem, recv_sem, peer):
        pltpu.make_async_remote_copy(
            src_ref=source, dst_ref=target, send_sem=send_sem, recv_sem=recv_sem,
            device_id=peer, device_id_type=MESH,
        ).start()

    def drain(ref, sem):
        pltpu.make_async_copy(ref, ref, sem).wait()

    load_ids.wait()
    load_rhs.wait()
    load_basis.wait()
    numbers = jnp.concatenate([ids[0], ids[1]], axis=1)
    places = ((numbers & 496) << 1) | ((numbers >> 9) << 4) | (numbers & 15)
    rows = lax.broadcasted_iota(jnp.int32, (NC, 2 * KC), 0)
    scatter = jnp.where(rows == places, 1.0, 0.0).astype(BF16)
    terms = []
    for s in range(2):
        high, rest = split(rhs[s, 0])
        terms.append(dot(basis[s, 0], high) + dot(basis[s, 0], rest))
    high, rest = split(jnp.concatenate(terms, axis=0))
    local_sums = dot(scatter, high) + dot(scatter, rest)
    sbuf[...] = local_sums.astype(BF16).reshape(32, 32, R)

    pl.semaphore_wait(barrier, len(greeted))
    for slot, offset in enumerate(PLANE):
        block, peer = plane_peer(offset)
        send(sbuf.at[block], rbuf.at[slot], rs_send, rs_recv, peer)
    load_cinv.wait()
    for dz in RING:
        send(cz.at[z], cz.at[z], cz_send, cz_recv, ring_peer(dz))

    load_inv.wait()
    heads = [rhs[s, 0].astype(BF16) for s in range(2)]
    for s in range(2):
        edge = dot(inv[s, 0, OWN:, :], heads[s]).astype(BF16).reshape(4, H, R)
        mbuf[s] = edge
        marg[1 - s, s] = edge[1 - s]
    send(mbuf.at[1, 1], marg.at[0, 0], m_send, m_recv, east)
    send(mbuf.at[0, 0], marg.at[1, 1], m_send, m_recv, west)
    send(mbuf.at[:, 3], marg.at[:, 2], m_send, m_recv, north)
    send(mbuf.at[:, 2], marg.at[:, 3], m_send, m_recv, south)
    for s in range(2):
        corr[s] = dot(inv[s, 0, :OWN, :], heads[s])
    load_spill.wait()
    for s in range(2):
        listed = spill[s, 0]
        listed = jnp.concatenate([listed[d : d + 1] for d in range(4)], axis=1)
        owned = lax.broadcasted_iota(jnp.int32, (OWN, 4 * H), 0)
        spread_mat[s] = jnp.where(owned == listed, 1.0, 0.0).astype(BF16)
        basis_t[s] = basis[s, 0].T
    pick = jnp.where(rows == numbers, 1.0, 0.0).astype(BF16)

    drain(cz.at[0:7], cz_recv)
    cf[y, core, x] = jnp.concatenate([cz[i].astype(F32) for i in range(ZS)], axis=0).astype(BF16)
    for d in (2, 1, 3):
        send(cf.at[y, core, x, 0:16], cf.at[y, core, x, 0:16], c2_send.at[0], c2_recv.at[0], x_peer(d))
        send(cf.at[y, core, x, 16:32], cf.at[y, core, x, 16:32], c2_send.at[1], c2_recv.at[1], y_peer(d))

    drain(rbuf, rs_recv)
    total = sbuf[mine].astype(F32)
    for slot in range(31):
        total = total + rbuf[slot].astype(F32)
    zs[...] = total.astype(BF16)
    for slot, dz in enumerate(RING):
        send(zs, zr.at[slot], z_send, z_recv, ring_peer(dz))

    drain(cf.at[0, 0, 0:3, 0:16], c2_recv.at[0])
    drain(cf.at[0, 0, 0:3, 0:16], c2_recv.at[1])
    for d in (2, 1, 3):
        send(cf.at[y, core, :, 0:16], cf.at[y, core, :, 0:16], c3_send.at[0], c3_recv.at[0], y_peer(d))
        send(cf.at[:, core, x, 16:32], cf.at[:, core, x, 16:32], c3_send.at[1], c3_recv.at[1], x_peer(d))

    def kept(values):
        return [
            (jnp.where(gx > 0, values[0, 0], 0), values[0, 1], jnp.where(gy > 0, values[0, 2], 0),
             jnp.where(gy < 15, values[0, 3], 0)),
            (values[1, 0], jnp.where(gx < 15, values[1, 1], 0), jnp.where(gy > 0, values[1, 2], 0),
             jnp.where(gy < 15, values[1, 3], 0)),
        ]

    drain(mbuf.at[:, 0:3], m_recv)
    received = kept(marg)
    for s in range(2):
        corr[s] = corr[s] + dot(spread_mat[s], jnp.concatenate(received[s], axis=0))

    drain(zr, z_recv)
    total = total.astype(BF16).astype(F32)
    for slot in range(7):
        total = total + zr[slot].astype(F32)
    low[mine] = total.astype(BF16)
    for offset in PLANE:
        send(low.at[mine], low.at[mine], ag_send, ag_recv, plane_peer(offset)[1])

    drain(cf.at[0:3, 0, :, 0:16], c3_recv.at[0])
    drain(cf.at[0:3, 0, :, 0:16], c3_recv.at[1])
    send(cf.at[:, core], cf.at[:, core], c4_send, c4_recv, partner)
    drain(cf.at[:, 0], c4_recv)
    wsel[...] = dot(cf[...].reshape(NC, NC), pick).astype(BF16)

    load_op.wait()
    drain(low.at[0:31], ag_recv)
    picked = dot_first(wsel[...], low[...].reshape(NC, R))
    for s in range(2):
        high, rest = split(picked[s * KC : (s + 1) * KC])
        value = corr[s] + (dot(basis_t[s], high) + dot(basis_t[s], rest))
        out_sol[s, 0] = value
        heads[s] = value.astype(BF16)
        edge = dot(op[s, 0, OWN:, :], heads[s]).astype(BF16).reshape(4, H, R)
        mbuf2[s] = edge
        marg2[1 - s, s] = edge[1 - s]
    send(mbuf2.at[1, 1], marg2.at[0, 0], n_send, n_recv, east)
    send(mbuf2.at[0, 0], marg2.at[1, 1], n_send, n_recv, west)
    send(mbuf2.at[:, 3], marg2.at[:, 2], n_send, n_recv, north)
    send(mbuf2.at[:, 2], marg2.at[:, 3], n_send, n_recv, south)
    store_sol = pltpu.make_async_copy(out_sol, sol_hbm, store_sem.at[0])
    store_sol.start()
    for s in range(2):
        corr[s] = rhs[s, 0] - dot(op[s, 0, :OWN, :], heads[s])
    drain(mbuf2.at[:, 0:3], n_recv)
    received = kept(marg2)
    for s in range(2):
        out_res[s, 0] = corr[s] - dot(spread_mat[s], jnp.concatenate(received[s], axis=0))
    store_res = pltpu.make_async_copy(out_res, res_hbm, store_sem.at[1])
    store_res.start()

    drain(rbuf, rs_send)
    drain(zr, z_send)
    drain(low.at[0:31], ag_send)
    drain(cz.at[0:7], cz_send)
    for i in range(2):
        drain(cf.at[0, 0, 0:3, 0:16], c2_send.at[i])
        drain(cf.at[0:3, 0, :, 0:16], c3_send.at[i])
    drain(cf.at[:, 0], c4_send)
    drain(mbuf.at[:, 0:3], m_send)
    drain(mbuf2.at[:, 0:3], n_send)
    store_sol.wait()
    store_res.wait()


def body(adjoint_rhs, local_inverse, local_operator, spill_rows, coarse_basis, coarse_ids, coarse_inverse):
    anywhere = pl.BlockSpec(memory_space=pl.ANY)
    dma = pltpu.SemaphoreType.DMA
    out = jax.ShapeDtypeStruct(adjoint_rhs.shape, F32)
    return pl.pallas_call(
        kernel,
        out_shape=(out, out),
        in_specs=[anywhere] * 7,
        out_specs=(anywhere, anywhere),
        scratch_shapes=[
            pltpu.VMEM(adjoint_rhs.shape, F32),
            pltpu.VMEM(local_inverse.shape, BF16),
            pltpu.VMEM(local_operator.shape, BF16),
            pltpu.VMEM(spill_rows.shape, jnp.int32),
            pltpu.VMEM(coarse_basis.shape, BF16),
            pltpu.VMEM(coarse_ids.shape, jnp.int32),
            pltpu.VMEM((ZS, 4, NC), BF16),
            pltpu.VMEM((4, 2, 4, 32, NC), BF16),
            pltpu.VMEM((32, 32, R), BF16),
            pltpu.VMEM((31, 32, R), BF16),
            pltpu.VMEM((32, R), BF16),
            pltpu.VMEM((7, 32, R), BF16),
            pltpu.VMEM((32, 32, R), BF16),
            pltpu.VMEM((2, 4, H, R), BF16),
            pltpu.VMEM((2, 4, H, R), BF16),
            pltpu.VMEM((2, 4, H, R), BF16),
            pltpu.VMEM((2, 4, H, R), BF16),
            pltpu.VMEM((2, OWN, 4 * H), BF16),
            pltpu.VMEM((2, OWN, KC), BF16),
            pltpu.VMEM((NC, 2 * KC), BF16),
            pltpu.VMEM((2, OWN, R), F32),
            pltpu.VMEM(adjoint_rhs.shape, F32),
            pltpu.VMEM(adjoint_rhs.shape, F32),
            dma((7,)),
            dma(()), dma(()), dma(()), dma(()), dma(()), dma(()),
            dma(()), dma(()), dma((2,)), dma((2,)), dma((2,)), dma((2,)), dma(()), dma(()),
            dma(()), dma(()), dma(()), dma(()), dma((2,)),
        ],
        compiler_params=pltpu.CompilerParams(
            collective_id=0, has_side_effects=True, vmem_limit_bytes=48 * 1024 * 1024
        ),
    )(adjoint_rhs, local_inverse, local_operator, spill_rows, coarse_basis, coarse_ids, coarse_inverse)


def solution(mesh):
    in_specs = (
        P("gx", "gy", None, None),
        P("gx", "gy", None, None),
        P("gx", "gy", None, None),
        P("gx", "gy", None, None),
        P("gx", "gy", None, None),
        P("gx", "gy", None),
        P(("gx", "gy"), None),
    )
    out_specs = (P("gx", "gy", None, None), P("gx", "gy", None, None))
    return jax.shard_map(body, mesh=mesh, in_specs=in_specs, out_specs=out_specs, check_vma=False)
```

time: 504 us -> 46.7 us (0.09); the launches traced: 495 us -> 46.4 us
  waiting for transfers between devices: 244 us -> 0 us
  other arithmetic: 110 us -> 0 us
  blocking collectives: 82.9 us -> 0 us
  Pallas kernels: 0 us -> 38 us
  starting transfers between devices: 17.9 us -> 0 us
  matrix products: 14.2 us -> 0 us
  between operations: 14.3 us -> 0.65 us
    psum x1 -> x0, waiting for transfers between devices: 233 us -> none  [body(): coarse_sol = lax.psum(partial_sol, ('gx', 'gy'))]
    scatter-add x2 -> x0, other arithmetic: 105 us -> none  [add_rows(): return owned_rows.at[indices].add(values)]
    unnamed x1 -> x0, blocking collectives: 82.9 us -> none
    pallas_call x0 -> x1, Pallas kernels: none -> 38 us  [body(): pl.pallas_call(kernel, out_shape=(out, out), in_specs=[anywhere] * 7, out...]
    ppermute x8 -> x0, starting transfers between devices: 17.9 us -> none  [the longest x4 11 us: with_halo(): lax.ppermute(lax.slice_in_dim(block, block.shape[dim] - width, None, axis...]
    dot_general x7 -> x0, matrix products: 14.2 us -> none  [the longest x1 3.29 us: body(): jnp.einsum('sln,snr->slr', operators, correction.astype(jnp.bfloat16), pr...]
    ppermute x8 -> x0, waiting for transfers between devices: 11.6 us -> none  [the longest x4 11.2 us: with_halo(): lax.ppermute(lax.slice_in_dim(block, 0, width, axis=dim), axis, backward)]
    slice x5 -> x0, local copies, waits for them, and re-layouts: 6.2 us -> none  [the longest x2 4.39 us: spread(): owned_rows = extended[:, :owned_count]]
  transfers between devices with their start and end apart: 9 -> 0, of which waited for: 4 -> 0; matrix products, arithmetic and copies ran while one was open for 2% -> 0% of each run, Pallas kernels for 0% -> 0%
where the time goes in v1:
time: 46.7 us; the launch traced here: 46.4 us
  Pallas kernels  38 us (81%)
  local copies, waits for them, and re-layouts  7.76 us (17%)
  between operations  0.65 us (1%)
    pallas_call x1, Pallas kernels, body(): pl.pallas_call(kernel, out_shape=(out, out), in_specs=[anywhere] * 7, out...  38 us
    unnamed x14, local copies, waits for them, and re-layouts  7.76 us

profile of v1, /device:TPU:1, one launch (start us, length us, event | category | flops | bytes accessed | tf_op | source)
XLA Modules:
  0.0 46.4 jit_solution(9513821120210765217)
XLA Ops:
  0.6 0.0 copy-start
  0.6 1.9 %copy-done = bf16[2,1,1024,768]{3,2,1,0:T(8,128)(2,1)S(1)} copy-done((bf16[2,1,1024,768]{3,2,1,0:T(8,128)(2,1)S(1)}, bf16[2,1,1024,768]{3,2,1,0:T(8,128)(2,1)}, u32[]{:S(2)}) %copy-start) | copy-done | bytes 3145752
  2.5 0.0 copy-start.1
  2.5 1.1 %copy-done.1 = f32[2,1,768,128]{3,2,1,0:T(8,128)S(1)} copy-done((f32[2,1,768,128]{3,2,1,0:T(8,128)S(1)}, f32[2,1,768,128]{3,2,1,0:T(8,128)}, u32[]{:S(2)}) %copy-start.1) | copy-done | bytes 786456
  3.7 0.0 copy-start.2
  3.7 0.9 %copy-done.2 = bf16[2,1,64,768]{3,2,1,0:T(8,128)(2,1)S(1)} copy-done((bf16[2,1,64,768]{3,2,1,0:T(8,128)(2,1)S(1)}, bf16[2,1,64,768]{3,2,1,0:T(8,128)(2,1)}, u32[]{:S(2)}) %copy-start.2) | copy-done | bytes 196632
  4.6 0.0 copy-start.3
  4.6 0.7 %copy-done.3 = bf16[4,1024]{1,0:T(4,128)(2,1)S(1)} copy-done((bf16[4,1024]{1,0:T(4,128)(2,1)S(1)}, bf16[4,1024]{1,0:T(4,128)(2,1)}, u32[]{:S(2)}) %copy-start.3) | copy-done | bytes 8216
  5.3 0.0 copy-start.4
  5.3 0.7 %copy-done.4 = s32[2,1,4,64]{3,2,1,0:T(4,128)S(1)} copy-done((s32[2,1,4,64]{3,2,1,0:T(4,128)S(1)}, s32[2,1,4,64]{3,2,1,0:T(4,128)}, u32[]{:S(2)}) %copy-start.4) | copy-done | bytes 2072
  6.0 0.0 copy-start.5
  6.0 0.7 %copy-done.5 = s32[2,1,64]{2,1,0:T(1,128)S(1)} copy-done((s32[2,1,64]{2,1,0:T(1,128)S(1)}, s32[2,1,64]{2,1,0:T(1,128)}, u32[]{:S(2)}) %copy-start.5) | copy-done | bytes 536
  6.6 38.0 %shard_map.86 = (f32[2,1,768,128]{3,2,1,0:T(8,128)S(1)}, f32[2,1,768,128]{3,2,1,0:T(8,128)S(1)}) custom-call(f32[2,1,768,128]{3,2,1,0:T(8,128)S(1)} %copy-done.1, bf16[2,1,1024,768]{3,2,1,0:T(8,128)(2,1)S(1)} %copy-done, bf16[2,1,1024,768]{3,2,1,0:T(8,128)(2,1)} %op_hbm.1, s32[2,1,4,64]{3,2,1,0:T(4,128)S(1)} %copy-done.4, ...), custom_call_target="tpu_custom_call" | custom-call | tf_op jit(solution)/shard_map/pallas_call | solution.py:248
  44.7 0.9 %copy.11 = f32[2,1,768,128]{3,2,1,0:T(8,128)} copy(f32[2,1,768,128]{3,2,1,0:T(8,128)S(1)} %get-tuple-element.4) | data formatting | bytes 1572864
  45.6 0.9 %copy.12 = f32[2,1,768,128]{3,2,1,0:T(8,128)} copy(f32[2,1,768,128]{3,2,1,0:T(8,128)S(1)} %get-tuple-element.5) | data formatting | bytes 1572864
Async XLA Ops:
  0.6 1.9 %copy-start = (bf16[2,1,1024,768]{3,2,1,0:T(8,128)(2,1)S(1)}, bf16[2,1,1024,768]{3,2,1,0:T(8,128)(2,1)}, u32[]{:S(2)}) copy-start(bf16[2,1,1024,768]{3,2,1,0:T(8,128)(2,1)} %inv_hbm.1) | copy-start | bytes 9437188
  2.5 1.1 %copy-start.1 = (f32[2,1,768,128]{3,2,1,0:T(8,128)S(1)}, f32[2,1,768,128]{3,2,1,0:T(8,128)}, u32[]{:S(2)}) copy-start(f32[2,1,768,128]{3,2,1,0:T(8,128)} %rhs_hbm.1) | copy-start | bytes 2359300
  3.7 0.9 %copy-start.2 = (bf16[2,1,64,768]{3,2,1,0:T(8,128)(2,1)S(1)}, bf16[2,1,64,768]{3,2,1,0:T(8,128)(2,1)}, u32[]{:S(2)}) copy-start(bf16[2,1,64,768]{3,2,1,0:T(8,128)(2,1)} %basis_hbm.1) | copy-start | bytes 589828
  4.6 0.7 %copy-start.3 = (bf16[4,1024]{1,0:T(4,128)(2,1)S(1)}, bf16[4,1024]{1,0:T(4,128)(2,1)}, u32[]{:S(2)}) copy-start(bf16[4,1024]{1,0:T(4,128)(2,1)} %cinv_hbm.1) | copy-start | bytes 24580
  5.3 0.7 %copy-start.4 = (s32[2,1,4,64]{3,2,1,0:T(4,128)S(1)}, s32[2,1,4,64]{3,2,1,0:T(4,128)}, u32[]{:S(2)}) copy-start(s32[2,1,4,64]{3,2,1,0:T(4,128)} %spill_hbm.1) | copy-start | bytes 6148
  6.0 0.7 %copy-start.5 = (s32[2,1,64]{2,1,0:T(1,128)S(1)}, s32[2,1,64]{2,1,0:T(1,128)}, u32[]{:S(2)}) copy-start(s32[2,1,64]{2,1,0:T(1,128)} %ids_hbm.1) | copy-start | bytes 1540

commit v2 on v1

--- a/solution.py
+++ b/solution.py
@@ -44,14 +44,14 @@
 
 def kernel(
     rhs_hbm, inv_hbm, op_hbm, spill_hbm, basis_hbm, ids_hbm, cinv_hbm,
-    sol_hbm, res_hbm,
+    out_sol, out_res,
     rhs, inv, op, spill, basis, ids, cz, cf,
     sbuf, rbuf, zs, zr, low,
-    mbuf, marg, mbuf2, marg2, spread_mat, basis_t, wsel,
-    corr, out_sol, out_res,
+    mbuf, marg, mbuf2, marg2, nids, spread_mat, basis_t, qmat, pick, wsel,
+    corr, prior,
     load_sem, rs_send, rs_recv, z_send, z_recv, ag_send, ag_recv,
     cz_send, cz_recv, c2_send, c2_recv, c3_send, c3_recv, c4_send, c4_recv,
-    m_send, m_recv, n_send, n_recv, store_sem,
+    m_send, m_recv, n_send, n_recv, i_send, i_recv,
 ):
     gx, gy = lax.axis_index("gx"), lax.axis_index("gy")
     core = lax.rem(gx, 2)
@@ -109,6 +109,20 @@
 
     def drain(ref, sem):
         pltpu.make_async_copy(ref, ref, sem).wait()
+
+    def exchange(source, target, send_sem, recv_sem):
+        send(source.at[1, 1], target.at[0, 0], send_sem, recv_sem, east)
+        send(source.at[0, 0], target.at[1, 1], send_sem, recv_sem, west)
+        send(source.at[:, 3], target.at[:, 2], send_sem, recv_sem, north)
+        send(source.at[:, 2], target.at[:, 3], send_sem, recv_sem, south)
+
+    def kept(values):
+        return [
+            (jnp.where(gx > 0, values[0, 0], 0), values[0, 1], jnp.where(gy > 0, values[0, 2], 0),
+             jnp.where(gy < 15, values[0, 3], 0)),
+            (values[1, 0], jnp.where(gx < 15, values[1, 1], 0), jnp.where(gy > 0, values[1, 2], 0),
+             jnp.where(gy < 15, values[1, 3], 0)),
+        ]
 
     load_ids.wait()
     load_rhs.wait()
@@ -132,6 +146,10 @@
     load_cinv.wait()
     for dz in RING:
         send(cz.at[z], cz.at[z], cz_send, cz_recv, ring_peer(dz))
+    send(ids.at[1], nids.at[0], i_send, i_recv, east)
+    send(ids.at[0], nids.at[1], i_send, i_recv, west)
+    send(ids, nids.at[2:4], i_send, i_recv, north)
+    send(ids, nids.at[4:6], i_send, i_recv, south)
 
     load_inv.wait()
     heads = [rhs[s, 0].astype(BF16) for s in range(2)]
@@ -139,10 +157,7 @@
         edge = dot(inv[s, 0, OWN:, :], heads[s]).astype(BF16).reshape(4, H, R)
         mbuf[s] = edge
         marg[1 - s, s] = edge[1 - s]
-    send(mbuf.at[1, 1], marg.at[0, 0], m_send, m_recv, east)
-    send(mbuf.at[0, 0], marg.at[1, 1], m_send, m_recv, west)
-    send(mbuf.at[:, 3], marg.at[:, 2], m_send, m_recv, north)
-    send(mbuf.at[:, 2], marg.at[:, 3], m_send, m_recv, south)
+    exchange(mbuf, marg, m_send, m_recv)
     for s in range(2):
         corr[s] = dot(inv[s, 0, :OWN, :], heads[s])
     load_spill.wait()
@@ -151,14 +166,27 @@
         listed = jnp.concatenate([listed[d : d + 1] for d in range(4)], axis=1)
         owned = lax.broadcasted_iota(jnp.int32, (OWN, 4 * H), 0)
         spread_mat[s] = jnp.where(owned == listed, 1.0, 0.0).astype(BF16)
-        basis_t[s] = basis[s, 0].T
-    pick = jnp.where(rows == numbers, 1.0, 0.0).astype(BF16)
+        basis_t[s] = jnp.concatenate([basis[s, 0], basis[s, 0]], axis=0).T
+    load_op.wait()
+    left = lax.broadcasted_iota(jnp.int32, (H, R), 1) < KC
+    for s in range(2):
+        edge = dot(op[s, 0, OWN:, :], basis_t[s]).reshape(4, H, R)
+        for d in range(4):
+            half = jnp.where(left if d in (1, 3) else ~left, edge[d], 0.0).astype(BF16)
+            mbuf2[s, d, 1] = half
+            if d == 1 - s:
+                marg2[1 - s, s, 1] = half
+        qmat[s, :, 0:R] = dot(op[s, 0, :OWN, :], basis_t[s]).astype(BF16)
 
     drain(cz.at[0:7], cz_recv)
     cf[y, core, x] = jnp.concatenate([cz[i].astype(F32) for i in range(ZS)], axis=0).astype(BF16)
+    first, second = slice(0, 16), slice(16, 32)
     for d in (2, 1, 3):
-        send(cf.at[y, core, x, 0:16], cf.at[y, core, x, 0:16], c2_send.at[0], c2_recv.at[0], x_peer(d))
-        send(cf.at[y, core, x, 16:32], cf.at[y, core, x, 16:32], c2_send.at[1], c2_recv.at[1], y_peer(d))
+        send(cf.at[y, core, x, first], cf.at[y, core, x, first], c2_send.at[0], c2_recv.at[0], x_peer(d))
+        send(cf.at[y, core, x, second], cf.at[y, core, x, second], c2_send.at[1], c2_recv.at[1], y_peer(d))
+    for d in (2, 1, 3):
+        send(cf.at[y, core, x, first], cf.at[y, core, x, first], c3_send.at[0], c3_recv.at[0], y_peer(d))
+        send(cf.at[y, core, x, second], cf.at[y, core, x, second], c3_send.at[1], c3_recv.at[1], x_peer(d))
 
     drain(rbuf, rs_recv)
     total = sbuf[mine].astype(F32)
@@ -168,24 +196,26 @@
     for slot, dz in enumerate(RING):
         send(zs, zr.at[slot], z_send, z_recv, ring_peer(dz))
 
-    drain(cf.at[0, 0, 0:3, 0:16], c2_recv.at[0])
-    drain(cf.at[0, 0, 0:3, 0:16], c2_recv.at[1])
-    for d in (2, 1, 3):
-        send(cf.at[y, core, :, 0:16], cf.at[y, core, :, 0:16], c3_send.at[0], c3_recv.at[0], y_peer(d))
-        send(cf.at[:, core, x, 16:32], cf.at[:, core, x, 16:32], c3_send.at[1], c3_recv.at[1], x_peer(d))
-
-    def kept(values):
-        return [
-            (jnp.where(gx > 0, values[0, 0], 0), values[0, 1], jnp.where(gy > 0, values[0, 2], 0),
-             jnp.where(gy < 15, values[0, 3], 0)),
-            (values[1, 0], jnp.where(gx < 15, values[1, 1], 0), jnp.where(gy > 0, values[1, 2], 0),
-             jnp.where(gy < 15, values[1, 3], 0)),
-        ]
-
     drain(mbuf.at[:, 0:3], m_recv)
     received = kept(marg)
     for s in range(2):
         corr[s] = corr[s] + dot(spread_mat[s], jnp.concatenate(received[s], axis=0))
+        heads[s] = corr[s].astype(BF16)
+        edge = dot(op[s, 0, OWN:, :], heads[s]).astype(BF16).reshape(4, H, R)
+        for d in range(4):
+            mbuf2[s, d, 0] = edge[d]
+        marg2[1 - s, s, 0] = edge[1 - s]
+    exchange(mbuf2, marg2, n_send, n_recv)
+
+    drain(cf.at[0, 0, 0:3, first], c2_recv.at[0])
+    drain(cf.at[0, 0, 0:3, first], c2_recv.at[1])
+    for other in (1, 2, 3):
+        xx, yy = lax.rem(x + other, XS), lax.rem(y + other, YS)
+        for d in (2, 1, 3):
+            send(cf.at[y, core, xx, first], cf.at[y, core, xx, first], c3_send.at[0], c3_recv.at[0], y_peer(d))
+            send(cf.at[yy, core, x, second], cf.at[yy, core, x, second], c3_send.at[1], c3_recv.at[1], x_peer(d))
+    for s in range(2):
+        prior[s] = rhs[s, 0] - dot(op[s, 0, :OWN, :], heads[s])
 
     drain(zr, z_recv)
     total = total.astype(BF16).astype(F32)
@@ -195,61 +225,79 @@
     for offset in PLANE:
         send(low.at[mine], low.at[mine], ag_send, ag_recv, plane_peer(offset)[1])
 
-    drain(cf.at[0:3, 0, :, 0:16], c3_recv.at[0])
-    drain(cf.at[0:3, 0, :, 0:16], c3_recv.at[1])
+    drain(nids, i_recv)
+    numbers = jnp.concatenate([ids[0], ids[1]] + [nids[i] for i in range(6)], axis=1)
+    rows = lax.broadcasted_iota(jnp.int32, (NC, 8 * KC), 0)
+    pick[...] = jnp.where(rows == numbers, 1.0, 0.0).astype(BF16)
+    drain(mbuf2.at[:, 0:3], n_recv)
+    for s in range(2):
+        arrived = [
+            jnp.where(gx > 0, marg2[0, 0], 0) if s == 0 else marg2[1, 0],
+            marg2[0, 1] if s == 0 else jnp.where(gx < 15, marg2[1, 1], 0),
+            jnp.where(gy > 0, marg2[s, 2], 0),
+            jnp.where(gy < 15, marg2[s, 3], 0),
+        ]
+        prior[s] = prior[s] - dot(spread_mat[s], jnp.concatenate([a[0] for a in arrived], axis=0))
+        for half in range(2):
+            pair = jnp.concatenate([arrived[2 * half][1], arrived[2 * half + 1][1]], axis=0)
+            lanes = slice(R * (half + 1), R * (half + 2))
+            qmat[s, :, lanes] = dot(spread_mat[s, :, R * half : R * (half + 1)], pair).astype(BF16)
+
+    drain(cf.at[0:3, 0, :, first], c3_recv.at[0])
+    drain(cf.at[0:3, 0, :, first], c3_recv.at[1])
     send(cf.at[:, core], cf.at[:, core], c4_send, c4_recv, partner)
     drain(cf.at[:, 0], c4_recv)
-    wsel[...] = dot(cf[...].reshape(NC, NC), pick).astype(BF16)
-
-    load_op.wait()
+    wsel[...] = dot(cf[...].reshape(NC, NC), pick[...]).astype(BF16).T
+
     drain(low.at[0:31], ag_recv)
-    picked = dot_first(wsel[...], low[...].reshape(NC, R))
+    picked = dot(wsel[...], low[...].reshape(NC, R))
+    parts = [picked[i * KC : (i + 1) * KC].astype(BF16) for i in range(8)]
+    beside = ((2, 1, 4, 6), (0, 3, 5, 7))
     for s in range(2):
         high, rest = split(picked[s * KC : (s + 1) * KC])
-        value = corr[s] + (dot(basis_t[s], high) + dot(basis_t[s], rest))
-        out_sol[s, 0] = value
-        heads[s] = value.astype(BF16)
-        edge = dot(op[s, 0, OWN:, :], heads[s]).astype(BF16).reshape(4, H, R)
-        mbuf2[s] = edge
-        marg2[1 - s, s] = edge[1 - s]
-    send(mbuf2.at[1, 1], marg2.at[0, 0], n_send, n_recv, east)
-    send(mbuf2.at[0, 0], marg2.at[1, 1], n_send, n_recv, west)
-    send(mbuf2.at[:, 3], marg2.at[:, 2], n_send, n_recv, north)
-    send(mbuf2.at[:, 2], marg2.at[:, 3], n_send, n_recv, south)
-    store_sol = pltpu.make_async_copy(out_sol, sol_hbm, store_sem.at[0])
-    store_sol.start()
-    for s in range(2):
-        corr[s] = rhs[s, 0] - dot(op[s, 0, :OWN, :], heads[s])
-    drain(mbuf2.at[:, 0:3], n_recv)
-    received = kept(marg2)
-    for s in range(2):
-        out_res[s, 0] = corr[s] - dot(spread_mat[s], jnp.concatenate(received[s], axis=0))
-    store_res = pltpu.make_async_copy(out_res, res_hbm, store_sem.at[1])
-    store_res.start()
+        both = jnp.concatenate([high, rest], axis=0)
+        out_sol[s, 0] = corr[s] + dot(basis_t[s], both)
+        stack = jnp.concatenate([both] + [parts[i] for i in beside[s]], axis=0)
+        out_res[s, 0] = prior[s] - dot(qmat[s], stack)
 
     drain(rbuf, rs_send)
     drain(zr, z_send)
     drain(low.at[0:31], ag_send)
     drain(cz.at[0:7], cz_send)
+    drain(nids, i_send)
     for i in range(2):
-        drain(cf.at[0, 0, 0:3, 0:16], c2_send.at[i])
-        drain(cf.at[0:3, 0, :, 0:16], c3_send.at[i])
+        drain(cf.at[0, 0, 0:3, first], c2_send.at[i])
+        drain(cf.at[0:3, 0, :, first], c3_send.at[i])
     drain(cf.at[:, 0], c4_send)
     drain(mbuf.at[:, 0:3], m_send)
     drain(mbuf2.at[:, 0:3], n_send)
-    store_sol.wait()
-    store_res.wait()
+
+
+def deliver(sol_ref, res_ref, sol_out, res_out, sem):
+    copies = [
+        pltpu.make_async_copy(sol_ref, sol_out, sem.at[0]),
+        pltpu.make_async_copy(res_ref, res_out, sem.at[1]),
+    ]
+    for copy in copies:
+        copy.start()
+    for copy in copies:
+        copy.wait()
 
 
 def body(adjoint_rhs, local_inverse, local_operator, spill_rows, coarse_basis, coarse_ids, coarse_inverse):
     anywhere = pl.BlockSpec(memory_space=pl.ANY)
+    hbm = pl.BlockSpec(memory_space=pltpu.HBM)
+    vmem = pl.BlockSpec(memory_space=pltpu.VMEM)
     dma = pltpu.SemaphoreType.DMA
     out = jax.ShapeDtypeStruct(adjoint_rhs.shape, F32)
-    return pl.pallas_call(
+    operands = (
+        adjoint_rhs, local_inverse, local_operator, spill_rows, coarse_basis, coarse_ids, coarse_inverse
+    )
+    results = pl.pallas_call(
         kernel,
         out_shape=(out, out),
-        in_specs=[anywhere] * 7,
-        out_specs=(anywhere, anywhere),
+        in_specs=[hbm] * 7,
+        out_specs=(vmem, vmem),
         scratch_shapes=[
             pltpu.VMEM(adjoint_rhs.shape, F32),
             pltpu.VMEM(local_inverse.shape, BF16),
@@ -266,23 +314,33 @@
             pltpu.VMEM((32, 32, R), BF16),
             pltpu.VMEM((2, 4, H, R), BF16),
             pltpu.VMEM((2, 4, H, R), BF16),
-            pltpu.VMEM((2, 4, H, R), BF16),
-            pltpu.VMEM((2, 4, H, R), BF16),
+            pltpu.VMEM((2, 4, 2, H, R), BF16),
+            pltpu.VMEM((2, 4, 2, H, R), BF16),
+            pltpu.VMEM((6, 1, KC), jnp.int32),
             pltpu.VMEM((2, OWN, 4 * H), BF16),
-            pltpu.VMEM((2, OWN, KC), BF16),
-            pltpu.VMEM((NC, 2 * KC), BF16),
+            pltpu.VMEM((2, OWN, R), BF16),
+            pltpu.VMEM((2, OWN, 3 * R), BF16),
+            pltpu.VMEM((NC, 8 * KC), BF16),
+            pltpu.VMEM((8 * KC, NC), BF16),
             pltpu.VMEM((2, OWN, R), F32),
-            pltpu.VMEM(adjoint_rhs.shape, F32),
-            pltpu.VMEM(adjoint_rhs.shape, F32),
+            pltpu.VMEM((2, OWN, R), F32),
             dma((7,)),
             dma(()), dma(()), dma(()), dma(()), dma(()), dma(()),
             dma(()), dma(()), dma((2,)), dma((2,)), dma((2,)), dma((2,)), dma(()), dma(()),
-            dma(()), dma(()), dma(()), dma(()), dma((2,)),
+            dma(()), dma(()), dma(()), dma(()), dma(()), dma(()),
         ],
         compiler_params=pltpu.CompilerParams(
             collective_id=0, has_side_effects=True, vmem_limit_bytes=48 * 1024 * 1024
         ),
-    )(adjoint_rhs, local_inverse, local_operator, spill_rows, coarse_basis, coarse_ids, coarse_inverse)
+    )(*[pltpu.with_memory_space_constraint(a, pltpu.HBM) for a in operands])
+    return pl.pallas_call(
+        deliver,
+        out_shape=(out, out),
+        in_specs=[anywhere] * 2,
+        out_specs=(hbm, hbm),
+        scratch_shapes=[dma((2,))],
+        compiler_params=pltpu.CompilerParams(vmem_limit_bytes=16 * 1024 * 1024),
+    )(*results)
 
 
 def solution(mesh):

time: 46.7 us -> 35.1 us (0.75)
  local copies, waits for them, and re-layouts: 7.76 us -> 0 us
  Pallas kernels: 38 us -> 34.4 us
    unnamed x14 -> x0, local copies, waits for them, and re-layouts: 7.76 us -> none
    pallas_call x1 -> x2, Pallas kernels: 38 us -> 34.4 us  [the longest x1 33.2 us: body(): pl.pallas_call(kernel, out_shape=(out, out), in_specs=[hbm] * 7, out_spec...]
where the time goes in v2:
time: 35.1 us; the launch traced here: 35 us
  Pallas kernels  34.4 us (98%)
  between operations  0.64 us (2%)
    pallas_call x1, Pallas kernels, body(): pl.pallas_call(kernel, out_shape=(out, out), in_specs=[hbm] * 7, out_spec...  33.2 us
    pallas_call x1, Pallas kernels, body(): pl.pallas_call(deliver, out_shape=(out, out), in_specs=[anywhere] * 2, ou...  1.16 us

profile of v2, /device:TPU:1, one launch (start us, length us, event | category | flops | bytes accessed | tf_op | source)
XLA Modules:
  0.0 35.0 jit_solution(9238014965854235720)
XLA Ops:
  0.6 33.2 %shard_map.86 = (f32[2,1,768,128]{3,2,1,0:T(8,128)S(1)}, f32[2,1,768,128]{3,2,1,0:T(8,128)S(1)}) custom-call(f32[2,1,768,128]{3,2,1,0:T(8,128)} %rhs_hbm.1, bf16[2,1,1024,768]{3,2,1,0:T(8,128)(2,1)} %inv_hbm.1, bf16[2,1,1024,768]{3,2,1,0:T(8,128)(2,1)} %op_hbm.1, s32[2,1,4,64]{3,2,1,0:T(4,128)} %spill_hbm.1, bf16[2,1,64,768]{3,2,1,0:T(8,128)(2,1)} %basis_hbm.1, ...), custom_call_target="tpu_custom_call" | custom-call | tf_op jit(solution)/shard_map/pallas_call | solution.py:296
  33.9 1.2 %shard_map.87 = (f32[2,1,768,128]{3,2,1,0:T(8,128)}, f32[2,1,768,128]{3,2,1,0:T(8,128)}) custom-call(f32[2,1,768,128]{3,2,1,0:T(8,128)S(1)} %get-tuple-element.4.sol_ref, f32[2,1,768,128]{3,2,1,0:T(8,128)S(1)} %get-tuple-element.5.res_ref), custom_call_target="tpu_custom_call" | custom-call | tf_op jit(solution)/shard_map/pallas_call | solution.py:336

commit v3 on v2

--- a/solution.py
+++ b/solution.py
@@ -44,16 +44,16 @@
 
 def kernel(
     rhs_hbm, inv_hbm, op_hbm, spill_hbm, basis_hbm, ids_hbm, cinv_hbm,
-    out_sol, out_res,
+    corr, prior, basis_t, qmat, picked,
     rhs, inv, op, spill, basis, ids, cz, cf,
     sbuf, rbuf, zs, zr, low,
-    mbuf, marg, mbuf2, marg2, nids, spread_mat, basis_t, qmat, pick, wsel,
-    corr, prior,
+    mbuf, marg, mbuf2, marg2, nids, spread_mat, pick, wsel, lists, trade,
     load_sem, rs_send, rs_recv, z_send, z_recv, ag_send, ag_recv,
     cz_send, cz_recv, c2_send, c2_recv, c3_send, c3_recv, c4_send, c4_recv,
-    m_send, m_recv, n_send, n_recv, i_send, i_recv,
+    m_send, m_recv, n_send, n_recv, i_send, i_recv, l_send, l_recv,
 ):
     gx, gy = lax.axis_index("gx"), lax.axis_index("gy")
+
     core = lax.rem(gx, 2)
     y = lax.rem(lax.div(gx, 2), YS)
     x = lax.div(gy, 4)
@@ -92,14 +92,15 @@
     load_rhs = load(rhs_hbm, rhs, 1)
     load_basis = load(basis_hbm, basis, 2)
     load_cinv = load(cinv_hbm, cz.at[z], 3)
-    load_inv = load(inv_hbm, inv, 4)
-    load_spill = load(spill_hbm, spill, 5)
-    load_op = load(op_hbm, op, 6)
+
+    def signal(semaphore, peer):
+        pl.semaphore_signal(semaphore, inc=1, device_id=peer, device_id_type=MESH)
 
     barrier = pltpu.get_barrier_semaphore()
-    greeted = [plane_peer(o)[1] for o in PLANE] + [ring_peer(d) for d in RING] + [east, west, north, south]
+    ring = [ring_peer(d) for d in RING]
+    greeted = [plane_peer(o)[1] for o in PLANE] + ring + [east, west, north, south]
     for peer in greeted:
-        pl.semaphore_signal(barrier, inc=1, device_id=peer, device_id_type=MESH)
+        signal(barrier, peer)
 
     def send(source, target, send_sem, recv_sem, peer):
         pltpu.make_async_remote_copy(
@@ -127,6 +128,9 @@
     load_ids.wait()
     load_rhs.wait()
     load_basis.wait()
+    load_inv = load(inv_hbm, inv, 4)
+    load_spill = load(spill_hbm, spill, 5)
+    load_op = load(op_hbm, op, 6)
     numbers = jnp.concatenate([ids[0], ids[1]], axis=1)
     places = ((numbers & 496) << 1) | ((numbers >> 9) << 4) | (numbers & 15)
     rows = lax.broadcasted_iota(jnp.int32, (NC, 2 * KC), 0)
@@ -144,20 +148,20 @@
         block, peer = plane_peer(offset)
         send(sbuf.at[block], rbuf.at[slot], rs_send, rs_recv, peer)
     load_cinv.wait()
-    for dz in RING:
-        send(cz.at[z], cz.at[z], cz_send, cz_recv, ring_peer(dz))
+    for peer in ring:
+        send(cz.at[z], cz.at[z], cz_send, cz_recv, peer)
     send(ids.at[1], nids.at[0], i_send, i_recv, east)
     send(ids.at[0], nids.at[1], i_send, i_recv, west)
     send(ids, nids.at[2:4], i_send, i_recv, north)
     send(ids, nids.at[4:6], i_send, i_recv, south)
 
     load_inv.wait()
-    heads = [rhs[s, 0].astype(BF16) for s in range(2)]
-    for s in range(2):
-        edge = dot(inv[s, 0, OWN:, :], heads[s]).astype(BF16).reshape(4, H, R)
+    for s in range(2):
+        edge = dot(inv[s, 0, OWN:, :], rhs[s, 0].astype(BF16)).astype(BF16).reshape(4, H, R)
         mbuf[s] = edge
         marg[1 - s, s] = edge[1 - s]
     exchange(mbuf, marg, m_send, m_recv)
+    heads = [rhs[s, 0].astype(BF16) for s in range(2)]
     for s in range(2):
         corr[s] = dot(inv[s, 0, :OWN, :], heads[s])
     load_spill.wait()
@@ -178,23 +182,25 @@
                 marg2[1 - s, s, 1] = half
         qmat[s, :, 0:R] = dot(op[s, 0, :OWN, :], basis_t[s]).astype(BF16)
 
+    first, second = slice(0, 16), slice(16, 32)
+
     drain(cz.at[0:7], cz_recv)
     cf[y, core, x] = jnp.concatenate([cz[i].astype(F32) for i in range(ZS)], axis=0).astype(BF16)
-    first, second = slice(0, 16), slice(16, 32)
+    upper, lower = cf.at[y, core, x, first], cf.at[y, core, x, second]
     for d in (2, 1, 3):
-        send(cf.at[y, core, x, first], cf.at[y, core, x, first], c2_send.at[0], c2_recv.at[0], x_peer(d))
-        send(cf.at[y, core, x, second], cf.at[y, core, x, second], c2_send.at[1], c2_recv.at[1], y_peer(d))
+        send(upper, upper, c2_send.at[0], c2_recv.at[0], x_peer(d))
+        send(lower, lower, c2_send.at[1], c2_recv.at[1], y_peer(d))
     for d in (2, 1, 3):
-        send(cf.at[y, core, x, first], cf.at[y, core, x, first], c3_send.at[0], c3_recv.at[0], y_peer(d))
-        send(cf.at[y, core, x, second], cf.at[y, core, x, second], c3_send.at[1], c3_recv.at[1], x_peer(d))
+        send(upper, upper, c3_send.at[0], c3_recv.at[0, d - 1], y_peer(d))
+        send(lower, lower, c3_send.at[1], c3_recv.at[1, d - 1], x_peer(d))
 
     drain(rbuf, rs_recv)
     total = sbuf[mine].astype(F32)
     for slot in range(31):
         total = total + rbuf[slot].astype(F32)
     zs[...] = total.astype(BF16)
-    for slot, dz in enumerate(RING):
-        send(zs, zr.at[slot], z_send, z_recv, ring_peer(dz))
+    for slot, peer in enumerate(ring):
+        send(zs, zr.at[slot], z_send, z_recv, peer)
 
     drain(mbuf.at[:, 0:3], m_recv)
     received = kept(marg)
@@ -212,23 +218,30 @@
     for other in (1, 2, 3):
         xx, yy = lax.rem(x + other, XS), lax.rem(y + other, YS)
         for d in (2, 1, 3):
-            send(cf.at[y, core, xx, first], cf.at[y, core, xx, first], c3_send.at[0], c3_recv.at[0], y_peer(d))
-            send(cf.at[yy, core, x, second], cf.at[yy, core, x, second], c3_send.at[1], c3_recv.at[1], x_peer(d))
+            upper, lower = cf.at[y, core, xx, first], cf.at[yy, core, x, second]
+            send(upper, upper, c3_send.at[0], c3_recv.at[0, d - 1], y_peer(d))
+            send(lower, lower, c3_send.at[1], c3_recv.at[1, d - 1], x_peer(d))
+
     for s in range(2):
         prior[s] = rhs[s, 0] - dot(op[s, 0, :OWN, :], heads[s])
+    drain(nids, i_recv)
+    lists[0] = jnp.concatenate([ids[0], ids[1]] + [nids[i] for i in range(6)], axis=1)
+    send(lists.at[0], lists.at[1], l_send, l_recv, partner)
+    rows = lax.broadcasted_iota(jnp.int32, (NC, 8 * KC), 0)
+    pick[:, 0 : 8 * KC] = jnp.where(rows == lists[0], 1.0, 0.0).astype(BF16)
 
     drain(zr, z_recv)
     total = total.astype(BF16).astype(F32)
     for slot in range(7):
         total = total + zr[slot].astype(F32)
-    low[mine] = total.astype(BF16)
+    slot_here = y * 4 + x
+    low[slot_here] = total.astype(BF16)
     for offset in PLANE:
-        send(low.at[mine], low.at[mine], ag_send, ag_recv, plane_peer(offset)[1])
-
-    drain(nids, i_recv)
-    numbers = jnp.concatenate([ids[0], ids[1]] + [nids[i] for i in range(6)], axis=1)
-    rows = lax.broadcasted_iota(jnp.int32, (NC, 8 * KC), 0)
-    pick[...] = jnp.where(rows == numbers, 1.0, 0.0).astype(BF16)
+        if offset[2] == 0:
+            send(low.at[slot_here], low.at[slot_here], ag_send, ag_recv, plane_peer(offset)[1])
+
+    drain(lists.at[0], l_recv)
+    pick[:, 8 * KC :] = jnp.where(rows == lists[1], 1.0, 0.0).astype(BF16)
     drain(mbuf2.at[:, 0:3], n_recv)
     for s in range(2):
         arrived = [
@@ -243,49 +256,55 @@
             lanes = slice(R * (half + 1), R * (half + 2))
             qmat[s, :, lanes] = dot(spread_mat[s, :, R * half : R * (half + 1)], pair).astype(BF16)
 
-    drain(cf.at[0:3, 0, :, first], c3_recv.at[0])
-    drain(cf.at[0:3, 0, :, first], c3_recv.at[1])
-    send(cf.at[:, core], cf.at[:, core], c4_send, c4_recv, partner)
-    drain(cf.at[:, 0], c4_recv)
-    wsel[...] = dot(cf[...].reshape(NC, NC), pick[...]).astype(BF16).T
-
-    drain(low.at[0:31], ag_recv)
-    picked = dot(wsel[...], low[...].reshape(NC, R))
-    parts = [picked[i * KC : (i + 1) * KC].astype(BF16) for i in range(8)]
-    beside = ((2, 1, 4, 6), (0, 3, 5, 7))
-    for s in range(2):
-        high, rest = split(picked[s * KC : (s + 1) * KC])
-        both = jnp.concatenate([high, rest], axis=0)
-        out_sol[s, 0] = corr[s] + dot(basis_t[s], both)
-        stack = jnp.concatenate([both] + [parts[i] for i in beside[s]], axis=0)
-        out_res[s, 0] = prior[s] - dot(qmat[s], stack)
+    for d in (1, 3, 2):
+        drain(cf.at[0, 0, :, first], c3_recv.at[0, d - 1])
+        drain(cf.at[0, 0, :, first], c3_recv.at[1, d - 1])
+    for part in (1, 0):
+        chosen = dot(cf[:, core].reshape(NC // 2, NC), pick[:, part * 8 * KC : (part + 1) * 8 * KC]).astype(BF16)
+        for i in range(4):
+            wsel[part, :, i * R : (i + 1) * R] = chosen[i * R : (i + 1) * R].T
+
+    drain(low.at[0:15], ag_recv)
+    summed = low[...].reshape(NC // 2, R)
+    trade[0] = dot(wsel[1], summed).astype(BF16)
+    send(trade.at[0], trade.at[1], c4_send, c4_recv, partner)
+    ours = dot(wsel[0], summed)
+    drain(trade.at[0], c4_recv)
+    picked[...] = ours + trade[1].astype(F32)
 
     drain(rbuf, rs_send)
     drain(zr, z_send)
-    drain(low.at[0:31], ag_send)
+    drain(low.at[0:15], ag_send)
     drain(cz.at[0:7], cz_send)
     drain(nids, i_send)
     for i in range(2):
         drain(cf.at[0, 0, 0:3, first], c2_send.at[i])
         drain(cf.at[0:3, 0, :, first], c3_send.at[i])
-    drain(cf.at[:, 0], c4_send)
+    drain(lists.at[0], l_send)
+    drain(trade.at[0], c4_send)
     drain(mbuf.at[:, 0:3], m_send)
     drain(mbuf2.at[:, 0:3], n_send)
 
 
-def deliver(sol_ref, res_ref, sol_out, res_out, sem):
-    copies = [
-        pltpu.make_async_copy(sol_ref, sol_out, sem.at[0]),
-        pltpu.make_async_copy(res_ref, res_out, sem.at[1]),
-    ]
-    for copy in copies:
-        copy.start()
+def finish(corr, prior, basis_t, qmat, picked, sol_out, res_out, sol, res, sem):
+    parts = [picked[i * KC : (i + 1) * KC].astype(BF16) for i in range(8)]
+    beside = ((2, 1, 4, 6), (0, 3, 5, 7))
+    copies = []
+    for s in range(2):
+        high, rest = split(picked[s * KC : (s + 1) * KC])
+        both = jnp.concatenate([high, rest], axis=0)
+        stack = jnp.concatenate([both] + [parts[i] for i in beside[s]], axis=0)
+        res[s] = prior[s] - dot(qmat[s], stack)
+        copies.append(pltpu.make_async_copy(res.at[s], res_out.at[s, 0], sem.at[2 * s]))
+        copies[-1].start()
+        sol[s] = corr[s] + dot(basis_t[s], both)
+        copies.append(pltpu.make_async_copy(sol.at[s], sol_out.at[s, 0], sem.at[2 * s + 1]))
+        copies[-1].start()
     for copy in copies:
         copy.wait()
 
 
 def body(adjoint_rhs, local_inverse, local_operator, spill_rows, coarse_basis, coarse_ids, coarse_inverse):
-    anywhere = pl.BlockSpec(memory_space=pl.ANY)
     hbm = pl.BlockSpec(memory_space=pltpu.HBM)
     vmem = pl.BlockSpec(memory_space=pltpu.VMEM)
     dma = pltpu.SemaphoreType.DMA
@@ -295,9 +314,15 @@
     )
     results = pl.pallas_call(
         kernel,
-        out_shape=(out, out),
+        out_shape=(
+            jax.ShapeDtypeStruct((2, OWN, R), F32),
+            jax.ShapeDtypeStruct((2, OWN, R), F32),
+            jax.ShapeDtypeStruct((2, OWN, R), BF16),
+            jax.ShapeDtypeStruct((2, OWN, 3 * R), BF16),
+            jax.ShapeDtypeStruct((8 * KC, R), F32),
+        ),
         in_specs=[hbm] * 7,
-        out_specs=(vmem, vmem),
+        out_specs=(vmem,) * 5,
         scratch_shapes=[
             pltpu.VMEM(adjoint_rhs.shape, F32),
             pltpu.VMEM(local_inverse.shape, BF16),
@@ -311,34 +336,32 @@
             pltpu.VMEM((31, 32, R), BF16),
             pltpu.VMEM((32, R), BF16),
             pltpu.VMEM((7, 32, R), BF16),
-            pltpu.VMEM((32, 32, R), BF16),
+            pltpu.VMEM((16, 32, R), BF16),
             pltpu.VMEM((2, 4, H, R), BF16),
             pltpu.VMEM((2, 4, H, R), BF16),
             pltpu.VMEM((2, 4, 2, H, R), BF16),
             pltpu.VMEM((2, 4, 2, H, R), BF16),
             pltpu.VMEM((6, 1, KC), jnp.int32),
             pltpu.VMEM((2, OWN, 4 * H), BF16),
-            pltpu.VMEM((2, OWN, R), BF16),
-            pltpu.VMEM((2, OWN, 3 * R), BF16),
-            pltpu.VMEM((NC, 8 * KC), BF16),
-            pltpu.VMEM((8 * KC, NC), BF16),
-            pltpu.VMEM((2, OWN, R), F32),
-            pltpu.VMEM((2, OWN, R), F32),
+            pltpu.VMEM((NC, 16 * KC), BF16),
+            pltpu.VMEM((2, 8 * KC, NC // 2), BF16),
+            pltpu.VMEM((2, 1, 8 * KC), jnp.int32),
+            pltpu.VMEM((2, 8 * KC, R), BF16),
             dma((7,)),
             dma(()), dma(()), dma(()), dma(()), dma(()), dma(()),
-            dma(()), dma(()), dma((2,)), dma((2,)), dma((2,)), dma((2,)), dma(()), dma(()),
-            dma(()), dma(()), dma(()), dma(()), dma(()), dma(()),
+            dma(()), dma(()), dma((2,)), dma((2,)), dma((2,)), dma((2, 3)), dma(()), dma(()),
+            dma(()), dma(()), dma(()), dma(()), dma(()), dma(()), dma(()), dma(()),
         ],
         compiler_params=pltpu.CompilerParams(
             collective_id=0, has_side_effects=True, vmem_limit_bytes=48 * 1024 * 1024
         ),
     )(*[pltpu.with_memory_space_constraint(a, pltpu.HBM) for a in operands])
     return pl.pallas_call(
-        deliver,
+        finish,
         out_shape=(out, out),
-        in_specs=[anywhere] * 2,
+        in_specs=[vmem] * 5,
         out_specs=(hbm, hbm),
-        scratch_shapes=[dma((2,))],
+        scratch_shapes=[pltpu.VMEM((2, OWN, R), F32), pltpu.VMEM((2, OWN, R), F32), dma((4,))],
         compiler_params=pltpu.CompilerParams(vmem_limit_bytes=16 * 1024 * 1024),
     )(*results)
 

time: 35.1 us -> 33.6 us (0.957)
  Pallas kernels: 34.4 us -> 32.8 us
    pallas_call x2, Pallas kernels: 34.4 us -> 32.8 us  [the longest x1 31.3 us: body(): pl.pallas_call(kernel, out_shape=(jax.ShapeDtypeStruct((2, OWN, R), F32),...]
where the time goes in v3:
time: 33.6 us; the launch traced here: 33.5 us
  Pallas kernels  32.8 us (98%)
  between operations  0.64 us (2%)
    pallas_call x1, Pallas kernels, body(): pl.pallas_call(kernel, out_shape=(jax.ShapeDtypeStruct((2, OWN, R), F32),...  31.3 us
    pallas_call x1, Pallas kernels, body(): pl.pallas_call(finish, out_shape=(out, out), in_specs=[vmem] * 5, out_spe...  1.53 us

profile of v3, /device:TPU:1, one launch (start us, length us, event | category | flops | bytes accessed | tf_op | source)
XLA Modules:
  0.0 33.5 jit_solution(6842210992882790736)
XLA Ops:
  0.6 31.3 %shard_map.86 = (f32[2,768,128]{2,1,0:T(8,128)S(1)}, f32[2,768,128]{2,1,0:T(8,128)S(1)}, bf16[2,768,128]{2,1,0:T(8,128)(2,1)S(1)}, bf16[2,768,384]{2,1,0:T(8,128)(2,1)S(1)}, f32[512,128]{1,0:T(8,128)S(1)}) custom-call(f32[2,1,768,128]{3,2,1,0:T(8,128)} %rhs_hbm.1, bf16[2,1,1024,768]{3,2,1,0:T(8,128)(2,1)} %inv_hbm.1, bf16[2,1,1024,768]{3,2,1,0:T(8,128)(2,1)} %op_hbm.1, ...), custom_call_target="tpu_custom_call" | custom-call | tf_op jit(solution)/shard_map/pallas_call | solution.py:315
  31.9 1.5 %shard_map.87 = (f32[2,1,768,128]{3,2,1,0:T(8,128)}, f32[2,1,768,128]{3,2,1,0:T(8,128)}) custom-call(f32[2,768,128]{2,1,0:T(8,128)S(1)} %get-tuple-element.7.corr, f32[2,768,128]{2,1,0:T(8,128)S(1)} %get-tuple-element.8.prior, bf16[2,768,128]{2,1,0:T(8,128)(2,1)S(1)} %get-tuple-element.9.basis_t, bf16[2,768,384]{2,1,0:T(8,128)(2,1)S(1)} %get-tuple-element.10.qmat, ...), custom_call_target="tpu_custom_call" | custom-call | tf_op jit(solution)/shard_map/pallas_call | solution.py:359

commit v4 on v3

--- a/solution.py
+++ b/solution.py
@@ -222,14 +222,6 @@
             send(upper, upper, c3_send.at[0], c3_recv.at[0, d - 1], y_peer(d))
             send(lower, lower, c3_send.at[1], c3_recv.at[1, d - 1], x_peer(d))
 
-    for s in range(2):
-        prior[s] = rhs[s, 0] - dot(op[s, 0, :OWN, :], heads[s])
-    drain(nids, i_recv)
-    lists[0] = jnp.concatenate([ids[0], ids[1]] + [nids[i] for i in range(6)], axis=1)
-    send(lists.at[0], lists.at[1], l_send, l_recv, partner)
-    rows = lax.broadcasted_iota(jnp.int32, (NC, 8 * KC), 0)
-    pick[:, 0 : 8 * KC] = jnp.where(rows == lists[0], 1.0, 0.0).astype(BF16)
-
     drain(zr, z_recv)
     total = total.astype(BF16).astype(F32)
     for slot in range(7):
@@ -240,6 +232,13 @@
         if offset[2] == 0:
             send(low.at[slot_here], low.at[slot_here], ag_send, ag_recv, plane_peer(offset)[1])
 
+    drain(nids, i_recv)
+    lists[0] = jnp.concatenate([ids[0], ids[1]] + [nids[i] for i in range(6)], axis=1)
+    send(lists.at[0], lists.at[1], l_send, l_recv, partner)
+    rows = lax.broadcasted_iota(jnp.int32, (NC, 8 * KC), 0)
+    pick[:, 0 : 8 * KC] = jnp.where(rows == lists[0], 1.0, 0.0).astype(BF16)
+    for s in range(2):
+        prior[s] = rhs[s, 0] - dot(op[s, 0, :OWN, :], heads[s])
     drain(lists.at[0], l_recv)
     pick[:, 8 * KC :] = jnp.where(rows == lists[1], 1.0, 0.0).astype(BF16)
     drain(mbuf2.at[:, 0:3], n_recv)
@@ -266,11 +265,12 @@
 
     drain(low.at[0:15], ag_recv)
     summed = low[...].reshape(NC // 2, R)
-    trade[0] = dot(wsel[1], summed).astype(BF16)
-    send(trade.at[0], trade.at[1], c4_send, c4_recv, partner)
-    ours = dot(wsel[0], summed)
+    for part in (slice(0, 4 * KC), slice(4 * KC, 8 * KC)):
+        trade[0, part] = dot(wsel[1, part], summed).astype(BF16)
+        send(trade.at[0, part], trade.at[1, part], c4_send, c4_recv, partner)
+    picked[...] = dot(wsel[0], summed)
     drain(trade.at[0], c4_recv)
-    picked[...] = ours + trade[1].astype(F32)
+    picked[...] += trade[1].astype(F32)
 
     drain(rbuf, rs_send)
     drain(zr, z_send)
@@ -290,16 +290,20 @@
     parts = [picked[i * KC : (i + 1) * KC].astype(BF16) for i in range(8)]
     beside = ((2, 1, 4, 6), (0, 3, 5, 7))
     copies = []
+
+    def put(source, target):
+        copies.append(pltpu.make_async_copy(source, target, sem.at[len(copies)]))
+        copies[-1].start()
+
     for s in range(2):
         high, rest = split(picked[s * KC : (s + 1) * KC])
         both = jnp.concatenate([high, rest], axis=0)
         stack = jnp.concatenate([both] + [parts[i] for i in beside[s]], axis=0)
-        res[s] = prior[s] - dot(qmat[s], stack)
-        copies.append(pltpu.make_async_copy(res.at[s], res_out.at[s, 0], sem.at[2 * s]))
-        copies[-1].start()
         sol[s] = corr[s] + dot(basis_t[s], both)
-        copies.append(pltpu.make_async_copy(sol.at[s], sol_out.at[s, 0], sem.at[2 * s + 1]))
-        copies[-1].start()
+        put(sol.at[s], sol_out.at[s, 0])
+        for part in (slice(0, OWN // 2), slice(OWN // 2, OWN)):
+            res[s, part] = prior[s, part] - dot(qmat[s, part], stack)
+            put(res.at[s, part], res_out.at[s, 0, part])
     for copy in copies:
         copy.wait()
 
@@ -361,7 +365,7 @@
         out_shape=(out, out),
         in_specs=[vmem] * 5,
         out_specs=(hbm, hbm),
-        scratch_shapes=[pltpu.VMEM((2, OWN, R), F32), pltpu.VMEM((2, OWN, R), F32), dma((4,))],
+        scratch_shapes=[pltpu.VMEM((2, OWN, R), F32), pltpu.VMEM((2, OWN, R), F32), dma((6,))],
         compiler_params=pltpu.CompilerParams(vmem_limit_bytes=16 * 1024 * 1024),
     )(*results)
 

time: 33.6 us -> 33 us (0.982)
  Pallas kernels: 32.8 us -> 32.2 us
    pallas_call x1, Pallas kernels: 31.3 us -> 30.8 us  [body(): pl.pallas_call(kernel, out_shape=(jax.ShapeDtypeStruct((2, OWN, R), F32),...]
where the time goes in v4:
time: 33 us; the launch traced here: 32.9 us
  Pallas kernels  32.2 us (98%)
  between operations  0.64 us (2%)
    pallas_call x1, Pallas kernels, body(): pl.pallas_call(kernel, out_shape=(jax.ShapeDtypeStruct((2, OWN, R), F32),...  30.8 us
    pallas_call x1, Pallas kernels, body(): pl.pallas_call(finish, out_shape=(out, out), in_specs=[vmem] * 5, out_spe...  1.43 us

profile of v4, /device:TPU:1, one launch (start us, length us, event | category | flops | bytes accessed | tf_op | source)
XLA Modules:
  0.0 32.9 jit_solution(10256453745356653530)
XLA Ops:
  0.6 30.8 %shard_map.86 = (f32[2,768,128]{2,1,0:T(8,128)S(1)}, f32[2,768,128]{2,1,0:T(8,128)S(1)}, bf16[2,768,128]{2,1,0:T(8,128)(2,1)S(1)}, bf16[2,768,384]{2,1,0:T(8,128)(2,1)S(1)}, f32[512,128]{1,0:T(8,128)S(1)}) custom-call(f32[2,1,768,128]{3,2,1,0:T(8,128)} %rhs_hbm.1, bf16[2,1,1024,768]{3,2,1,0:T(8,128)(2,1)} %inv_hbm.1, bf16[2,1,1024,768]{3,2,1,0:T(8,128)(2,1)} %op_hbm.1, ...), custom_call_target="tpu_custom_call" | custom-call | tf_op jit(solution)/shard_map/pallas_call | solution.py:319
  31.5 1.4 %shard_map.87 = (f32[2,1,768,128]{3,2,1,0:T(8,128)}, f32[2,1,768,128]{3,2,1,0:T(8,128)}) custom-call(f32[2,768,128]{2,1,0:T(8,128)S(1)} %get-tuple-element.7.corr, f32[2,768,128]{2,1,0:T(8,128)S(1)} %get-tuple-element.8.prior, bf16[2,768,128]{2,1,0:T(8,128)(2,1)S(1)} %get-tuple-element.9.basis_t, bf16[2,768,384]{2,1,0:T(8,128)(2,1)S(1)} %get-tuple-element.10.qmat, ...), custom_call_target="tpu_custom_call" | custom-call | tf_op jit(solution)/shard_map/pallas_call | solution.py:363

commit v5 on v4

--- a/solution.py
+++ b/solution.py
@@ -188,8 +188,8 @@
     cf[y, core, x] = jnp.concatenate([cz[i].astype(F32) for i in range(ZS)], axis=0).astype(BF16)
     upper, lower = cf.at[y, core, x, first], cf.at[y, core, x, second]
     for d in (2, 1, 3):
-        send(upper, upper, c2_send.at[0], c2_recv.at[0], x_peer(d))
-        send(lower, lower, c2_send.at[1], c2_recv.at[1], y_peer(d))
+        send(upper, upper, c2_send.at[0], c2_recv.at[0, d - 1], x_peer(d))
+        send(lower, lower, c2_send.at[1], c2_recv.at[1, d - 1], y_peer(d))
     for d in (2, 1, 3):
         send(upper, upper, c3_send.at[0], c3_recv.at[0, d - 1], y_peer(d))
         send(lower, lower, c3_send.at[1], c3_recv.at[1, d - 1], x_peer(d))
@@ -213,10 +213,10 @@
         marg2[1 - s, s, 0] = edge[1 - s]
     exchange(mbuf2, marg2, n_send, n_recv)
 
-    drain(cf.at[0, 0, 0:3, first], c2_recv.at[0])
-    drain(cf.at[0, 0, 0:3, first], c2_recv.at[1])
-    for other in (1, 2, 3):
-        xx, yy = lax.rem(x + other, XS), lax.rem(y + other, YS)
+    for back in (1, 3, 2):
+        drain(cf.at[0, 0, 0, first], c2_recv.at[0, back - 1])
+        drain(cf.at[0, 0, 0, first], c2_recv.at[1, back - 1])
+        xx, yy = lax.rem(x + XS - back, XS), lax.rem(y + YS - back, YS)
         for d in (2, 1, 3):
             upper, lower = cf.at[y, core, xx, first], cf.at[yy, core, x, second]
             send(upper, upper, c3_send.at[0], c3_recv.at[0, d - 1], y_peer(d))
@@ -353,7 +353,7 @@
             pltpu.VMEM((2, 8 * KC, R), BF16),
             dma((7,)),
             dma(()), dma(()), dma(()), dma(()), dma(()), dma(()),
-            dma(()), dma(()), dma((2,)), dma((2,)), dma((2,)), dma((2, 3)), dma(()), dma(()),
+            dma(()), dma(()), dma((2,)), dma((2, 3)), dma((2,)), dma((2, 3)), dma(()), dma(()),
             dma(()), dma(()), dma(()), dma(()), dma(()), dma(()), dma(()), dma(()),
         ],
         compiler_params=pltpu.CompilerParams(

time: 33 us -> 32.8 us (level)
  no operation moved by 1% of the time
where the time goes in v5:
time: 32.8 us; the launch traced here: 32.7 us
  Pallas kernels  32 us (98%)
  between operations  0.64 us (2%)
    pallas_call x1, Pallas kernels, body(): pl.pallas_call(kernel, out_shape=(jax.ShapeDtypeStruct((2, OWN, R), F32),...  30.6 us
    pallas_call x1, Pallas kernels, body(): pl.pallas_call(finish, out_shape=(out, out), in_specs=[vmem] * 5, out_spe...  1.43 us

profile of v5, /device:TPU:1, one launch (start us, length us, event | category | flops | bytes accessed | tf_op | source)
XLA Modules:
  0.0 32.7 jit_solution(3242487693942175321)
XLA Ops:
  0.6 30.6 %shard_map.86 = (f32[2,768,128]{2,1,0:T(8,128)S(1)}, f32[2,768,128]{2,1,0:T(8,128)S(1)}, bf16[2,768,128]{2,1,0:T(8,128)(2,1)S(1)}, bf16[2,768,384]{2,1,0:T(8,128)(2,1)S(1)}, f32[512,128]{1,0:T(8,128)S(1)}) custom-call(f32[2,1,768,128]{3,2,1,0:T(8,128)} %rhs_hbm.1, bf16[2,1,1024,768]{3,2,1,0:T(8,128)(2,1)} %inv_hbm.1, bf16[2,1,1024,768]{3,2,1,0:T(8,128)(2,1)} %op_hbm.1, ...), custom_call_target="tpu_custom_call" | custom-call | tf_op jit(solution)/shard_map/pallas_call | solution.py:319
  31.2 1.4 %shard_map.87 = (f32[2,1,768,128]{3,2,1,0:T(8,128)}, f32[2,1,768,128]{3,2,1,0:T(8,128)}) custom-call(f32[2,768,128]{2,1,0:T(8,128)S(1)} %get-tuple-element.7.corr, f32[2,768,128]{2,1,0:T(8,128)S(1)} %get-tuple-element.8.prior, bf16[2,768,128]{2,1,0:T(8,128)(2,1)S(1)} %get-tuple-element.9.basis_t, bf16[2,768,384]{2,1,0:T(8,128)(2,1)S(1)} %get-tuple-element.10.qmat, ...), custom_call_target="tpu_custom_call" | custom-call | tf_op jit(solution)/shard_map/pallas_call | solution.py:363

commit v6 on v5

--- a/solution.py
+++ b/solution.py
@@ -265,7 +265,7 @@
 
     drain(low.at[0:15], ag_recv)
     summed = low[...].reshape(NC // 2, R)
-    for part in (slice(0, 4 * KC), slice(4 * KC, 8 * KC)):
+    for part in (slice(0, 4 * KC), slice(4 * KC, 6 * KC), slice(6 * KC, 8 * KC)):
         trade[0, part] = dot(wsel[1, part], summed).astype(BF16)
         send(trade.at[0, part], trade.at[1, part], c4_send, c4_recv, partner)
     picked[...] = dot(wsel[0], summed)

time: 32.8 us -> 32.8 us (level)
  no operation moved by 1% of the time
where the time goes in v6:
time: 32.8 us; the launch traced here: 32.7 us
  Pallas kernels  32.1 us (98%)
  between operations  0.64 us (2%)
    pallas_call x1, Pallas kernels, body(): pl.pallas_call(kernel, out_shape=(jax.ShapeDtypeStruct((2, OWN, R), F32),...  30.7 us
    pallas_call x1, Pallas kernels, body(): pl.pallas_call(finish, out_shape=(out, out), in_specs=[vmem] * 5, out_spe...  1.43 us

profile of v6, /device:TPU:1, one launch (start us, length us, event | category | flops | bytes accessed | tf_op | source)
XLA Modules:
  0.0 32.7 jit_solution(9457425557445931278)
XLA Ops:
  0.6 30.7 %shard_map.86 = (f32[2,768,128]{2,1,0:T(8,128)S(1)}, f32[2,768,128]{2,1,0:T(8,128)S(1)}, bf16[2,768,128]{2,1,0:T(8,128)(2,1)S(1)}, bf16[2,768,384]{2,1,0:T(8,128)(2,1)S(1)}, f32[512,128]{1,0:T(8,128)S(1)}) custom-call(f32[2,1,768,128]{3,2,1,0:T(8,128)} %rhs_hbm.1, bf16[2,1,1024,768]{3,2,1,0:T(8,128)(2,1)} %inv_hbm.1, bf16[2,1,1024,768]{3,2,1,0:T(8,128)(2,1)} %op_hbm.1, ...), custom_call_target="tpu_custom_call" | custom-call | tf_op jit(solution)/shard_map/pallas_call | solution.py:319
  31.3 1.4 %shard_map.87 = (f32[2,1,768,128]{3,2,1,0:T(8,128)}, f32[2,1,768,128]{3,2,1,0:T(8,128)}) custom-call(f32[2,768,128]{2,1,0:T(8,128)S(1)} %get-tuple-element.7.corr, f32[2,768,128]{2,1,0:T(8,128)S(1)} %get-tuple-element.8.prior, bf16[2,768,128]{2,1,0:T(8,128)(2,1)S(1)} %get-tuple-element.9.basis_t, bf16[2,768,384]{2,1,0:T(8,128)(2,1)S(1)} %get-tuple-element.10.qmat, ...), custom_call_target="tpu_custom_call" | custom-call | tf_op jit(solution)/shard_map/pallas_call | solution.py:363
